TPU v7x, 32 devices: a whole 2x2x4 slice. The times are simulated.
32 devices in a mesh: seq: 8 (over y, x, core), head: 4 (over z).
Axes of the slice: x: 2, y: 2, z: 4, core: 2. Of those that a mesh axis runs over, the one named last changes fastest.
Arguments:
- inputs: bfloat16 [4096, 4096], P('seq'), may hold values from -6 to 6
- queries: bfloat16 [4096, 4096], P('seq', 'head'), may hold values from -6 to 6
- keys: bfloat16 [4096, 4096], P('seq', 'head'), may hold values from -6 to 6
- values: bfloat16 [4096, 4096], P('seq', 'head'), may hold values from -6 to 6
- out_grad: bfloat16 [4096, 4096], P('seq', 'head'), may hold values from -6 to 6
- value_weight: bfloat16 [4096, 4096], P('seq', 'head'), may hold values from -0.125 to 0.125
Outputs:
- grad_input: bfloat16 [4096, 4096], P('seq', 'head')
- grad_query: bfloat16 [4096, 4096], P('seq', 'head')
- grad_key: bfloat16 [4096, 4096], P('seq', 'head')
- grad_value: bfloat16 [4096, 4096], P('seq', 'head')
- grad_weight: float32 [4096, 4096], P('seq', 'head')
All inputs are finite; a program needn't handle non-finite values.
Results may differ from a plain program's by a relative error of at most 0.015.
Values may be sent and summed in bfloat16 or wider, within the bound.
A program may use at most 128 MiB of HBM per device.

v0:
```python
import math
import jax
import jax.numpy as jnp
from jax import lax
from jax.sharding import PartitionSpec as P

HEAD_DIM = 128


def carried_in(shard, axis, combine, identity, reverse):
    count, here = (lax.axis_size(axis), lax.axis_index(axis))
    everything = lax.all_gather(shard.astype(jnp.bfloat16), axis)
    start = jnp.broadcast_to(jnp.asarray(identity, shard.dtype), shard.shape)

    def lap(k, before):
        at = count - 1 - k if reverse else k
        reached = at > here if reverse else at < here
        new = combine(before, everything[at].astype(shard.dtype))
        return jnp.where(reached, new, before)

    return lax.fori_loop(0, count, lap, start)


def add_states(earlier, later):
    return earlier + later


def local(inputs, queries, keys, values, out_grad, value_weight):
    f32 = jnp.float32
    high = lax.Precision.HIGHEST
    rows = queries.shape[0]
    width = queries.shape[1]
    nheads = width // HEAD_DIM
    first = lax.axis_index("seq") * rows
    posit = (first + jnp.arange(rows, dtype=jnp.int32)).astype(f32)
    factor = 1.0 / jnp.sqrt(HEAD_DIM * (posit + 1.0))
    q3 = queries.reshape(rows, nheads, HEAD_DIM)
    k3 = keys.reshape(rows, nheads, HEAD_DIM)
    v3 = values.reshape(rows, nheads, HEAD_DIM)
    o3 = out_grad.reshape(rows, nheads, HEAD_DIM)
    o3wide = o3.astype(f32)
    state_kv = jnp.einsum("thi,thj->hij", k3, v3, preferred_element_type=f32)
    state_qo = jnp.einsum(
        "thi,thj->hij", q3.astype(f32), o3wide * factor[:, None, None], precision=high
    )
    empty_state = jnp.zeros_like(state_kv)
    prefix = carried_in(state_kv, "seq", add_states, empty_state, False)
    suffix = carried_in(state_qo, "seq", add_states, empty_state, True)
    index = jnp.arange(rows, dtype=jnp.int32)
    lower = (index[:, None] >= index[None, :])[None]
    score_qk = (
        jnp.einsum("thd,shd->hts", q3, k3, preferred_element_type=f32) * factor[None, :, None]
    )
    score_qk = jnp.where(lower, score_qk, 0.0).astype(jnp.bfloat16)
    score_ov = (
        jnp.einsum("thd,shd->hts", o3, v3, preferred_element_type=f32) * factor[None, :, None]
    )
    score_ov = jnp.where(lower, score_ov, 0.0).astype(jnp.bfloat16)
    dq = jnp.einsum("hts,shd->thd", score_ov, k3, preferred_element_type=f32)
    dq = dq + factor[:, None, None] * jnp.einsum("thj,hij->thi", o3wide, prefix, precision=high)
    dk = jnp.einsum("hts,thd->shd", score_ov, q3, preferred_element_type=f32)
    dk = dk + jnp.einsum("shj,hij->shi", v3.astype(f32), suffix, precision=high)
    dv = jnp.einsum("hts,thd->shd", score_qk, o3, preferred_element_type=f32)
    dv = dv + jnp.einsum("shi,hij->shj", k3.astype(f32), suffix, precision=high)
    grad_query = dq.reshape(rows, width).astype(jnp.bfloat16)
    grad_key = dk.reshape(rows, width).astype(jnp.bfloat16)
    grad_value = dv.reshape(rows, width).astype(jnp.bfloat16)
    both_last = (((1,), (1,)), ((), ()))
    partial_grad = lax.dot_general(
        grad_value,
        lax.all_gather(value_weight, "seq", axis=0, tiled=True),
        both_last,
        preferred_element_type=f32,
    )
    grad_input = lax.psum_scatter(
        partial_grad.astype(jnp.bfloat16), "head", scatter_dimension=1, tiled=True
    )
    wscale = 1.0 / math.sqrt(rows * lax.axis_size("seq"))
    product = lax.dot_general(
        inputs, grad_value, (((0,), (0,)), ((), ())), preferred_element_type=f32
    )
    grad_weight = lax.psum_scatter(
        (product * wscale).astype(jnp.bfloat16), "seq", scatter_dimension=0, tiled=True
    ).astype(jnp.float32)
    return (grad_input, grad_query, grad_key, grad_value, grad_weight)


def solution(mesh):
    in_specs = (
        P("seq", None),
        P("seq", "head"),
        P("seq", "head"),
        P("seq", "head"),
        P("seq", "head"),
        P("seq", "head"),
    )
    out_specs = (
        P("seq", "head"),
        P("seq", "head"),
        P("seq", "head"),
        P("seq", "head"),
        P("seq", "head"),
    )
    return jax.shard_map(local, mesh=mesh, in_specs=in_specs, out_specs=out_specs, check_vma=False)
```

profile of v0, /device:TPU:0, one launch (start us, length us, event | category | flops | bytes accessed | tf_op | source)
XLA Modules:
  0.0 291.6 jit_solution(2182478048408645564)
XLA Ops:
  7.2 2.4 copy.48
  9.6 1.5 copy.49
  11.1 2.4 fusion.16
  13.5 0.8 copy.32
  14.4 0.0 all-gather.6.cloned.1.call-start
  14.4 0.7 all-gather.6.cloned.1.call-update
  15.1 0.0 all-gather.10.cloned.1.call-start
  15.2 2.4 convolution_convert_fusion.1
  17.7 0.0 reduce-scatter.5.cloned.1.call-start
  17.7 0.1 iota_compare_fusion
  17.8 5.0 %fusion.1 = f32[8,512,128]{1,2,0:T(8,128)} fusion(bf16[512,8,128]{0,2,1:T(8,128)(2,1)} %bitcast.99, f32[512]{0:T(512)S(1)} %multiply_rsqrt_fusion, pred[512,512]{1,0:T(8,128)(4,1)S(1)} %iota_compare_fusion, bf16[512,8,128]{0,2,1:T(8,128)(2,1)S(1)} %bitcast.96, bf16[512,1024]{1,0:T(8,128)(2,1)} %param.12), kind=kOutput, calls=%fused_computation.7 | convolution fusion | flops 1080033280 | bytes 5507072 | tf_op jit(solution)/shard_map/hts,thd->shd/dot_general | solution.py:63
  22.8 22.2 %all-gather.8.cloned.1.call-done = bf16[64,128,128]{2,1,0:T(8,128)(2,1)} async-done(((bf16[8,128,128]{2,1,0:T(8,128)(2,1)}), bf16[64,128,128]{2,1,0:T(8,128)(2,1)}) %all-gather.8.cloned.1.call-update) | async-done | bytes 2097168 | tf_op jit(solution)/shard_map/all_gather | solution.py:12
  45.0 10.1 %while.30 = (s32[]{:T(128)}, f32[8,128,128]{2,1,0:T(8,128)S(1)}, s32[]{:T(128)}, bf16[8,8,128,128]{3,2,1,0:T(8,128)(2,1)}, s32[]{:T(128)}, /*index=5*/s32[]{:T(128)}, s32[]{:T(128)}, s32[]{:T(128)}) while((s32[]{:T(128)}, f32[8,128,128]{2,1,0:T(8,128)S(1)}, s32[]{:T(128)}, bf16[8,8,128,128]{3,2,1,0:T(8,128)(2,1)}, s32[]{:T(128)}, ...), condition=%wide.region_1.2_spmd.clone, body=%wide.region_0.1_spmd.clone.sunk | while | flops 524296 | bytes 1310883 | solution.py:21
  45.0 1.2 add_select_fusion.4
  46.3 1.2 add_select_fusion.4
  47.6 1.2 add_select_fusion.4
  48.8 1.2 add_select_fusion.4
  50.1 1.2 add_select_fusion.4
  51.3 1.2 add_select_fusion.4
  52.6 1.3 add_select_fusion.4
  53.9 1.3 add_select_fusion.4
  55.2 3.4 %fusion.9 = bf16[512,8,128]{0,2,1:T(8,128)(2,1)S(1)} fusion(f32[8,512,128]{1,2,0:T(8,128)} %fusion.1, f32[8,128,128]{2,1,0:T(8,128)S(1)} %get-tuple-element.194, bf16[512,1024]{1,0:T(8,128)(2,1)} %param.12), kind=kOutput, calls=%fused_computation.17 | convolution fusion | flops 806354944 | bytes 4718592 | tf_op jit(solution)/shard_map/shi,hij->shj/dot_general | solution.py:64
  58.6 1.0 copy-done.3
  59.6 6.8 %fusion = bf16[4096,1024]{0,1:T(8,128)(2,1)} fusion(bf16[512,1024]{0,1:T(8,128)(2,1)S(1)} %bitcast.102, bf16[512,4096]{1,0:T(8,128)(2,1)S(1)} %copy-done.4), kind=kOutput, calls=%fused_computation.5 | convolution fusion | flops 4303355904 | bytes 13631488 | tf_op jit(solution)/shard_map/dot_general | solution.py:79
  66.4 0.2 reduce-scatter.3.cloned.1.call-start
  66.6 34.6 %all-gather.6.cloned.1.call-done = bf16[4096,1024]{1,0:T(8,128)(2,1)} async-done(((bf16[512,1024]{1,0:T(8,128)(2,1)}), bf16[4096,1024]{1,0:T(8,128)(2,1)}) %all-gather.6.cloned.1.call-update) | async-done | bytes 8388624 | tf_op jit(solution)/shard_map/all_gather | solution.py:71
  101.2 10.2 %convolution_convert_fusion = bf16[512,4096]{1,0:T(8,128)(2,1)} fusion(bf16[512,1024]{0,1:T(8,128)(2,1)} %bitcast.103, bf16[4096,1024]{1,0:T(8,128)(2,1)} %all-gather.6.cloned.1.call-done), kind=kOutput, calls=%fused_computation.6 | convolution fusion | flops 4297064448 | bytes 13631488 | tf_op jit(solution)/shard_map/dot_general | solution.py:69
  111.5 3.1 %select_convert_fusion = bf16[8,512,512]{2,1,0:T(8,128)(2,1)S(1)} fusion(f32[512]{0:T(512)S(1)} %multiply_rsqrt_fusion, pred[512,512]{1,0:T(8,128)(4,1)S(1)} %iota_compare_fusion, bf16[512,8,128]{0,2,1:T(8,128)(2,1)} %bitcast.100, bf16[512,1024]{1,0:T(8,128)(2,1)S(1)} %copy-done), kind=kOutput, calls=%fused_computation.3 | convolution fusion | flops 543162368 | bytes 6555648 | tf_op jit(solution)/shard_map/thd,shd->hts/dot_general | solution.py:56
  114.6 2.8 fusion.24
  117.4 2.1 fusion.38
  119.5 2.4 copy.45
  121.9 9.1 %all-gather.10.cloned.1.call-done = bf16[64,128,128]{2,1,0:T(8,128)(2,1)} async-done(((bf16[8,128,128]{2,1,0:T(8,128)(2,1)}), bf16[64,128,128]{2,1,0:T(8,128)(2,1)}) %all-gather.10.cloned.1.call-update) | async-done | bytes 2097168 | tf_op jit(solution)/shard_map/all_gather | solution.py:12
  130.9 10.0 %while.31 = (s32[]{:T(128)}, f32[8,128,128]{2,1,0:T(8,128)S(1)}, s32[]{:T(128)}, bf16[8,8,128,128]{3,2,1,0:T(8,128)(2,1)}, s32[]{:T(128)}, /*index=5*/s32[]{:T(128)}) while((s32[]{:T(128)}, f32[8,128,128]{2,1,0:T(8,128)S(1)}, s32[]{:T(128)}, bf16[8,8,128,128]{3,2,1,0:T(8,128)(2,1)}, s32[]{:T(128)}, /*index=5*/s32[]{:T(128)}) %tuple.90), condition=%wide.region_4.5_spmd.clone, body=%wide.region_3.4_spmd.clone.sunk | while | flops 524292 | bytes 1310821 | solution.py:21
  130.9 1.2 add_select_fusion.5
  132.2 1.2 add_select_fusion.5
  133.4 1.2 add_select_fusion.5
  134.7 1.2 add_select_fusion.5
  135.9 1.2 add_select_fusion.5
  137.2 1.2 add_select_fusion.5
  138.5 1.2 add_select_fusion.5
  139.7 1.2 add_select_fusion.5
  141.0 4.0 %fusion.8 = bf16[512,8,128]{0,2,1:T(8,128)(2,1)} fusion(f32[8,512,128]{1,2,0:T(8,128)} %fusion.24, f32[8,128,128]{2,1,0:T(8,128)S(1)} %get-tuple-element.195, bf16[512,8,128]{0,2,1:T(8,128)(2,1)S(1)} %bitcast.101, f32[512]{0:T(512)S(1)} %multiply_rsqrt_fusion), kind=kOutput, calls=%fused_computation.15 | convolution fusion | flops 806879232 | bytes 4720640 | tf_op jit(solution)/shard_map/thj,hij->thi/dot_general | solution.py:60
  145.0 2.4 copy.43
  147.5 3.0 %fusion.7 = bf16[512,8,128]{0,2,1:T(8,128)(2,1)S(1)} fusion(f32[8,512,128]{1,2,0:T(8,128)} %fusion.38, f32[8,128,128]{2,1,0:T(8,128)S(1)} %get-tuple-element.194, bf16[512,1024]{1,0:T(8,128)(2,1)S(1)} %copy-done), kind=kOutput, calls=%fused_computation.13 | convolution fusion | flops 806354944 | bytes 4718592 | tf_op jit(solution)/shard_map/shj,hij->shi/dot_general | solution.py:62
  150.4 1.3 copy.44
  151.8 53.8 %reduce-scatter.5.cloned.1.call-done = bf16[512,1024]{0,1:T(8,128)(2,1)} async-done(((bf16[4096,1024]{0,1:T(8,128)(2,1)}), bf16[512,1024]{0,1:T(8,128)(2,1)}) %reduce-scatter.5.cloned.1.call-update) | async-done | bytes 1048592 | tf_op jit(solution)/shard_map/reduce_scatter | solution.py:82
  205.6 2.6 copy.46
  208.1 77.0 %reduce-scatter.3.cloned.1.call-done = bf16[512,1024]{1,0:T(8,128)(2,1)} async-done(((bf16[512,4096]{1,0:T(8,128)(2,1)}), bf16[512,1024]{1,0:T(8,128)(2,1)}) %reduce-scatter.3.cloned.1.call-update) | async-done | bytes 1048592 | tf_op jit(solution)/shard_map/reduce_scatter | solution.py:75
  (17 shorter events, 0.1 us)
Async XLA Ops:
  7.2 8.0 %copy-start = (bf16[512,1024]{1,0:T(8,128)(2,1)S(1)}, bf16[512,1024]{1,0:T(8,128)(2,1)}, u32[]{:S(2)}) copy-start(bf16[512,1024]{1,0:T(8,128)(2,1)} %param.13) | copy-start | bytes 3145732
  7.2 37.9 %all-gather.8.cloned.1.call-start = ((), (), s32[]{:S(2)}) async-start(), calls=%async_computation.5 | async-start | bytes 2359296 | tf_op jit(solution)/shard_map/all_gather | solution.py:12
  14.4 86.8 %all-gather.6.cloned.1.call-start = ((), (), s32[]{:S(2)}) async-start(), calls=%async_computation.2 | async-start | bytes 9437184 | tf_op jit(solution)/shard_map/all_gather | solution.py:71
  15.1 115.8 %all-gather.10.cloned.1.call-start = ((), (), s32[]{:S(2)}) async-start(), calls=%async_computation.6 | async-start | bytes 2359296 | tf_op jit(solution)/shard_map/all_gather | solution.py:12
  17.7 187.9 %reduce-scatter.5.cloned.1.call-start = ((), (), s32[]{:S(2)}) async-start(), calls=%async_computation.4 | async-start | bytes 9437184 | tf_op jit(solution)/shard_map/reduce_scatter | solution.py:82
  55.2 4.4 %copy-start.4 = (bf16[512,4096]{1,0:T(8,128)(2,1)S(1)}, bf16[512,4096]{1,0:T(8,128)(2,1)}, u32[]{:S(2)}) copy-start(bf16[512,4096]{1,0:T(8,128)(2,1)} %param.10) | copy-start | bytes 12582916
  58.6 1.0 copy-start.3
  66.4 218.7 %reduce-scatter.3.cloned.1.call-start = ((), (), s32[]{:S(2)}) async-start(), calls=%async_computation.3 | async-start | bytes 5242880 | tf_op jit(solution)/shard_map/reduce_scatter | solution.py:75
  111.5 3.1 %copy-start.2 = (bf16[512,1024]{1,0:T(8,128)(2,1)S(1)}, bf16[512,1024]{1,0:T(8,128)(2,1)}, u32[]{:S(2)}) copy-start(bf16[512,1024]{1,0:T(8,128)(2,1)} %param.12) | copy-start | bytes 3145732
  119.5 21.5 %copy-start.1 = (bf16[512,1024]{0,1:T(8,128)(2,1)S(1)}, bf16[512,1024]{0,1:T(8,128)(2,1)}, u32[]{:S(2)}) copy-start(bf16[512,1024]{0,1:T(8,128)(2,1)} %copy.48) | copy-start | bytes 3145732
Sparse Core Ops, SparseCore 0:
  14.5 30.4 all-gather.7
  46.9 54.2 all-gather.5
  103.1 27.7 all-gather.9
  134.2 71.2 reduce-scatter.4
  208.3 76.7 reduce-scatter.2
where the time goes:
time: 293 us; the launch traced here: 292 us
  waiting for transfers between devices  197 us (67%)
  matrix products  45.3 us (15%)
  other arithmetic  19.9 us (7%)
  local copies, waits for them, and re-layouts  14.3 us (5%)
  between operations  13.9 us (5%)
    reduce_scatter x1, waiting for transfers between devices, local(): lax.psum_scatter(partial_grad.astype(jnp.bfloat16), 'head', scatter_dimen...  77 us
    reduce_scatter x1, waiting for transfers between devices, local(): lax.psum_scatter((product * wscale).astype(jnp.bfloat16), 'seq', scatter_...  53.8 us
    all_gather x1, waiting for transfers between devices, local(): lax.all_gather(value_weight, 'seq', axis=0, tiled=True)  34.6 us
    all_gather x2, waiting for transfers between devices, carried_in(): everything = lax.all_gather(shard.astype(jnp.bfloat16), axis)  31.3 us
    select_n x16, other arithmetic, lap(): return jnp.where(reached, new, before)  19.8 us
    dot_general x1, matrix products, local(): lax.dot_general(grad_value, lax.all_gather(value_weight, 'seq', axis=0, t...  10.2 us
    unnamed x14, local copies, waits for them, and re-layouts  9.64 us
    dot_general x1, matrix products, local(): lax.dot_general(inputs, grad_value, (((0,), (0,)), ((), ())), preferred_e...  6.77 us
  transfers between devices with their start and end apart: 5, of which 5 were waited for; matrix products, arithmetic and copies ran while one was open for 25% of the time, Pallas kernels for 0%

commit v1 on v0

--- a/solution.py
+++ b/solution.py
@@ -5,6 +5,25 @@
 from jax.sharding import PartitionSpec as P
 
 HEAD_DIM = 128
+
+
+def gather_around(shard, axis, dim):
+    size, index, span = (lax.axis_size(axis), lax.axis_index(axis), shard.shape[dim])
+    right = [(i, (i + 1) % size) for i in range(size)]
+    behind = [(i, (i - 1) % size) for i in range(size)]
+    out = jnp.zeros((*shard.shape[:dim], size * span, *shard.shape[dim + 1 :]), shard.dtype)
+    out = lax.dynamic_update_slice_in_dim(out, shard, index * span, axis=dim)
+    from_left = from_right = shard
+    halfway = size // 2
+    for hop in range(1, halfway + 1):
+        from_left = lax.ppermute(from_left, axis, right)
+        out = lax.dynamic_update_slice_in_dim(out, from_left, (index - hop) % size * span, axis=dim)
+        if hop < size - halfway:
+            from_right = lax.ppermute(from_right, axis, behind)
+            out = lax.dynamic_update_slice_in_dim(
+                out, from_right, (index + hop) % size * span, axis=dim
+            )
+    return out
 
 
 def carried_in(shard, axis, combine, identity, reverse):
@@ -67,10 +86,7 @@
     grad_value = dv.reshape(rows, width).astype(jnp.bfloat16)
     both_last = (((1,), (1,)), ((), ()))
     partial_grad = lax.dot_general(
-        grad_value,
-        lax.all_gather(value_weight, "seq", axis=0, tiled=True),
-        both_last,
-        preferred_element_type=f32,
+        grad_value, gather_around(value_weight, "seq", 0), both_last, preferred_element_type=f32
     )
     grad_input = lax.psum_scatter(
         partial_grad.astype(jnp.bfloat16), "head", scatter_dimension=1, tiled=True

time: 293 us -> 284 us (0.969)
  waiting for transfers between devices: 197 us -> 173 us
  local copies, waits for them, and re-layouts: 14.3 us -> 23.7 us
  starting transfers between devices: 0.38 us -> 8.42 us
    ppermute x0 -> x7, waiting for transfers between devices: none -> 109 us  [the longest x4 106 us: gather_around(): from_left = lax.ppermute(from_left, axis, right)]
    reduce_scatter x1, waiting for transfers between devices: 53.8 us -> 0.01 us  [local(): lax.psum_scatter((product * wscale).astype(jnp.bfloat16), 'seq', scatter_...]
    reduce_scatter x1, waiting for transfers between devices: 77 us -> 41.3 us  [local(): lax.psum_scatter(partial_grad.astype(jnp.bfloat16), 'head', scatter_dimen...]
    all_gather x1 -> x0, waiting for transfers between devices: 34.6 us -> none  [local(): lax.all_gather(value_weight, 'seq', axis=0, tiled=True)]
    all_gather x2, waiting for transfers between devices: 31.3 us -> 23 us  [carried_in(): everything = lax.all_gather(shard.astype(jnp.bfloat16), axis)]
    ppermute x0 -> x7, starting transfers between devices: none -> 8.26 us  [the longest x3 7.96 us: gather_around(): from_right = lax.ppermute(from_right, axis, behind)]
    dynamic_update_slice x0 -> x8, local copies, waits for them, and re-layouts: none -> 5.75 us  [the longest x4 2.87 us: gather_around(): lax.dynamic_update_slice_in_dim(out, from_left, (index - hop) % size * sp...]
    dot_general x1, matrix products: 10.2 us -> 6.15 us  [local(): lax.dot_general(grad_value, gather_around(value_weight, 'seq', 0), both_l...]
  transfers between devices with their start and end apart: 5 -> 11, of which waited for: 5 -> 7; matrix products, arithmetic and copies ran while one was open for 25% -> 27% of each run, Pallas kernels for 0% -> 0%
where the time goes in v1:
time: 284 us; the launch traced here: 283 us
  waiting for transfers between devices  173 us (61%)
  matrix products  43.1 us (15%)
  local copies, waits for them, and re-layouts  23.7 us (8%)
  other arithmetic  19.9 us (7%)
  between operations  14 us (5%)
  starting transfers between devices  8.42 us (3%)
    ppermute x4, waiting for transfers between devices, gather_around(): from_left = lax.ppermute(from_left, axis, right)  106 us
    reduce_scatter x1, waiting for transfers between devices, local(): lax.psum_scatter(partial_grad.astype(jnp.bfloat16), 'head', scatter_dimen...  41.3 us
    all_gather x2, waiting for transfers between devices, carried_in(): everything = lax.all_gather(shard.astype(jnp.bfloat16), axis)  23 us
    select_n x16, other arithmetic, lap(): return jnp.where(reached, new, before)  19.8 us
    unnamed x28, local copies, waits for them, and re-layouts  12.2 us
    dot_general x1, matrix products, local(): lax.dot_general(inputs, grad_value, (((0,), (0,)), ((), ())), preferred_e...  8.92 us
    ppermute x3, starting transfers between devices, gather_around(): from_right = lax.ppermute(from_right, axis, behind)  7.96 us
    dot_general x1, matrix products, local(): lax.dot_general(grad_value, gather_around(value_weight, 'seq', 0), both_l...  6.15 us
  transfers between devices with their start and end apart: 11, of which 7 were waited for; matrix products, arithmetic and copies ran while one was open for 27% of the time, Pallas kernels for 0%

profile of v1, /device:TPU:0, one launch (start us, length us, event | category | flops | bytes accessed | tf_op | source)
XLA Modules:
  0.0 282.6 jit_solution(8096243304979797483)
XLA Ops:
  7.2 2.4 copy.48
  9.6 1.5 copy.49
  11.1 2.4 fusion.16
  14.4 2.5 convolution_convert_fusion.1
  17.1 5.0 %fusion.1 = f32[8,512,128]{1,2,0:T(8,128)} fusion(bf16[512,8,128]{0,2,1:T(8,128)(2,1)} %bitcast.99, f32[512]{0:T(512)S(1)} %multiply_rsqrt_fusion, pred[512,512]{1,0:T(8,128)(4,1)S(1)} %iota_compare_fusion, bf16[512,8,128]{0,2,1:T(8,128)(2,1)S(1)} %bitcast.96, bf16[512,1024]{1,0:T(8,128)(2,1)} %param.12), kind=kOutput, calls=%fused_computation.7 | convolution fusion | flops 1080033280 | bytes 5507072 | tf_op jit(solution)/shard_map/hts,thd->shd/dot_general | solution.py:82
  22.1 23.0 %all-gather.5.cloned.1.call-done = bf16[64,128,128]{2,1,0:T(8,128)(2,1)} async-done(((bf16[8,128,128]{2,1,0:T(8,128)(2,1)}), bf16[64,128,128]{2,1,0:T(8,128)(2,1)}) %all-gather.5.cloned.1.call-update) | async-done | bytes 2097168 | tf_op jit(solution)/shard_map/all_gather | solution.py:31
  45.0 10.1 %while.30 = (s32[]{:T(128)}, f32[8,128,128]{2,1,0:T(8,128)S(1)}, s32[]{:T(128)}, bf16[8,8,128,128]{3,2,1,0:T(8,128)(2,1)}, s32[]{:T(128)}, /*index=5*/s32[]{:T(128)}, s32[]{:T(128)}, s32[]{:T(128)}) while((s32[]{:T(128)}, f32[8,128,128]{2,1,0:T(8,128)S(1)}, s32[]{:T(128)}, bf16[8,8,128,128]{3,2,1,0:T(8,128)(2,1)}, s32[]{:T(128)}, ...), condition=%wide.region_1.2_spmd.clone, body=%wide.region_0.1_spmd.clone.sunk | while | flops 524296 | bytes 1310875 | solution.py:40
  46.3 1.2 add_select_fusion.4
  47.6 1.2 add_select_fusion.4
  48.8 1.2 add_select_fusion.4
  50.1 1.2 add_select_fusion.4
  51.4 1.2 add_select_fusion.4
  52.6 1.2 add_select_fusion.4
  53.9 1.2 add_select_fusion.4
  55.1 3.0 %fusion.9 = bf16[512,8,128]{0,2,1:T(8,128)(2,1)S(1)} fusion(f32[8,512,128]{1,2,0:T(8,128)} %fusion.1, f32[8,128,128]{2,1,0:T(8,128)S(1)} %get-tuple-element.194, bf16[512,1024]{1,0:T(8,128)(2,1)} %param.12), kind=kOutput, calls=%fused_computation.17 | convolution fusion | flops 806354944 | bytes 4718592 | tf_op jit(solution)/shard_map/shi,hij->shj/dot_general | solution.py:83
  59.1 8.9 %fusion = bf16[4096,1024]{0,1:T(8,128)(2,1)} fusion(bf16[512,1024]{0,1:T(8,128)(2,1)S(1)} %bitcast.102, bf16[512,4096]{1,0:T(8,128)(2,1)} %param.10), kind=kOutput, calls=%fused_computation.5 | convolution fusion | flops 4303355904 | bytes 13631488 | tf_op jit(solution)/shard_map/dot_general | solution.py:95
  68.4 2.4 collective-permute-start.1
  70.8 25.5 %collective-permute-done = bf16[512,1024]{1,0:T(8,128)(2,1)S(1)} collective-permute-done((bf16[512,1024]{1,0:T(8,128)(2,1)}, bf16[512,1024]{1,0:T(8,128)(2,1)S(1)}, u32[]{:S(2)}, u32[]{:S(2)}) %collective-permute-start) | collective-permute-done | bytes 1048608 | tf_op jit(solution)/shard_map/ppermute | solution.py:19
  97.3 2.6 collective-permute-start.3
  99.9 38.6 %collective-permute-done.2 = bf16[512,1024]{1,0:T(8,128)(2,1)S(1)} collective-permute-done((bf16[512,1024]{1,0:T(8,128)(2,1)S(1)}, bf16[512,1024]{1,0:T(8,128)(2,1)S(1)}, u32[]{:S(2)}, u32[]{:S(2)}) %collective-permute-start.2) | collective-permute-done | bytes 1048608 | tf_op jit(solution)/shard_map/ppermute | solution.py:19
  138.5 2.4 collective-permute-done.3
  140.9 2.9 %collective-permute-start.5 = (bf16[512,1024]{1,0:T(8,128)(2,1)}, bf16[512,1024]{1,0:T(8,128)(2,1)}, u32[]{:S(2)}, u32[]{:S(2)}) collective-permute-start(bf16[512,1024]{1,0:T(8,128)(2,1)} %collective-permute-done.3), channel_id=1, source_target_pairs={{0,28},{4,0},{8,4},{12,8},{16,12},{20,16},{24,20},{28,24},{1,29},{... | collective-permute-start | bytes 3145736 | tf_op jit(solution)/shard_map/ppermute | solution.py:22
  143.8 33.2 %collective-permute-done.4 = bf16[512,1024]{1,0:T(8,128)(2,1)} collective-permute-done((bf16[512,1024]{1,0:T(8,128)(2,1)S(1)}, bf16[512,1024]{1,0:T(8,128)(2,1)}, u32[]{:S(2)}, u32[]{:S(2)}) %collective-permute-start.4) | collective-permute-done | bytes 1048608 | tf_op jit(solution)/shard_map/ppermute | solution.py:19
  179.3 1.3 constant_dynamic-update-slice_fusion.3
  180.7 1.3 constant_dynamic-update-slice_fusion.2
  182.0 1.3 constant_dynamic-update-slice_fusion.1
  183.4 9.1 %collective-permute-done.6 = bf16[512,1024]{1,0:T(8,128)(2,1)} collective-permute-done((bf16[512,1024]{1,0:T(8,128)(2,1)}, bf16[512,1024]{1,0:T(8,128)(2,1)}, u32[]{:S(2)}, u32[]{:S(2)}) %collective-permute-start.6) | collective-permute-done | bytes 1048608 | tf_op jit(solution)/shard_map/ppermute | solution.py:19
  192.5 1.3 constant_dynamic-update-slice_fusion
  193.8 6.1 %convolution_convert_fusion = bf16[512,4096]{1,0:T(8,128)(2,1)} fusion(bf16[512,1024]{0,1:T(8,128)(2,1)S(1)} %bitcast.104, bf16[4096,1024]{1,0:T(8,128)(2,1)S(1)} %constant_dynamic-update-slice_fusion), kind=kOutput, calls=%fused_computation.6 | convolution fusion | flops 4297064448 | bytes 13631488 | tf_op jit(solution)/shard_map/dot_general | solution.py:88
  200.0 3.0 %select_convert_fusion = bf16[8,512,512]{2,1,0:T(8,128)(2,1)S(1)} fusion(f32[512]{0:T(512)S(1)} %multiply_rsqrt_fusion, pred[512,512]{1,0:T(8,128)(4,1)S(1)} %iota_compare_fusion, bf16[512,8,128]{0,2,1:T(8,128)(2,1)} %bitcast.100, bf16[512,1024]{1,0:T(8,128)(2,1)S(1)} %copy-done), kind=kOutput, calls=%fused_computation.3 | convolution fusion | flops 543162368 | bytes 6555648 | tf_op jit(solution)/shard_map/thd,shd->hts/dot_general | solution.py:75
  203.1 2.1 fusion.38
  205.1 2.8 fusion.24
  208.0 2.4 copy.45
  210.3 3.6 %fusion.7 = bf16[512,8,128]{0,2,1:T(8,128)(2,1)} fusion(f32[8,512,128]{1,2,0:T(8,128)} %fusion.38, f32[8,128,128]{2,1,0:T(8,128)S(1)} %get-tuple-element.194, bf16[512,1024]{1,0:T(8,128)(2,1)S(1)} %copy-done), kind=kOutput, calls=%fused_computation.13 | convolution fusion | flops 806354944 | bytes 4718592 | tf_op jit(solution)/shard_map/shj,hij->shi/dot_general | solution.py:81
  213.9 2.3 copy.44
  216.2 10.0 %while.31 = (s32[]{:T(128)}, f32[8,128,128]{2,1,0:T(8,128)S(1)}, s32[]{:T(128)}, bf16[8,8,128,128]{3,2,1,0:T(8,128)(2,1)}, s32[]{:T(128)}, /*index=5*/s32[]{:T(128)}) while((s32[]{:T(128)}, f32[8,128,128]{2,1,0:T(8,128)S(1)}, s32[]{:T(128)}, bf16[8,8,128,128]{3,2,1,0:T(8,128)(2,1)}, s32[]{:T(128)}, /*index=5*/s32[]{:T(128)}) %tuple.88), condition=%wide.region_4.5_spmd.clone, body=%wide.region_3.4_spmd.clone.sunk | while | flops 524292 | bytes 1310813 | solution.py:40
  216.2 1.2 add_select_fusion.5
  217.4 1.2 add_select_fusion.5
  218.7 1.2 add_select_fusion.5
  219.9 1.2 add_select_fusion.5
  221.2 1.2 add_select_fusion.5
  222.5 1.2 add_select_fusion.5
  223.7 1.2 add_select_fusion.5
  225.0 1.2 add_select_fusion.5
  226.2 3.7 %fusion.8 = bf16[512,8,128]{0,2,1:T(8,128)(2,1)} fusion(f32[8,512,128]{1,2,0:T(8,128)} %fusion.24, f32[8,128,128]{2,1,0:T(8,128)S(1)} %get-tuple-element.195, bf16[512,8,128]{0,2,1:T(8,128)(2,1)S(1)} %bitcast.101, f32[512]{0:T(512)S(1)} %multiply_rsqrt_fusion), kind=kOutput, calls=%fused_computation.15 | convolution fusion | flops 806879232 | bytes 4720640 | tf_op jit(solution)/shard_map/thj,hij->thi/dot_general | solution.py:79
  229.9 2.3 copy.43
  232.2 2.6 copy.46
  234.7 41.3 %reduce-scatter.3.cloned.1.call-done = bf16[512,1024]{1,0:T(8,128)(2,1)} async-done(((bf16[512,4096]{1,0:T(8,128)(2,1)}), bf16[512,1024]{1,0:T(8,128)(2,1)}) %reduce-scatter.3.cloned.1.call-update) | async-done | bytes 1048592 | tf_op jit(solution)/shard_map/reduce_scatter | solution.py:91
  (51 shorter events, 6.9 us)
Async XLA Ops:
  7.2 7.3 %copy-start = (bf16[512,1024]{1,0:T(8,128)(2,1)S(1)}, bf16[512,1024]{1,0:T(8,128)(2,1)}, u32[]{:S(2)}) copy-start(bf16[512,1024]{1,0:T(8,128)(2,1)} %param.13) | copy-start | bytes 3145732
  7.2 37.9 %all-gather.5.cloned.1.call-start = ((), (), s32[]{:S(2)}) async-start(), calls=%async_computation.4 | async-start | bytes 2359296 | tf_op jit(solution)/shard_map/all_gather | solution.py:31
  14.4 201.8 %all-gather.7.cloned.1.call-start = ((), (), s32[]{:S(2)}) async-start(), calls=%async_computation.5 | async-start | bytes 2359296 | tf_op jit(solution)/shard_map/all_gather | solution.py:31
  16.9 215.2 %reduce-scatter.5.cloned.1.call-start = ((), (), s32[]{:S(2)}) async-start(), calls=%async_computation.3 | async-start | bytes 9437184 | tf_op jit(solution)/shard_map/reduce_scatter | solution.py:98
  58.1 1.0 copy-start.3
  68.1 208.0 %reduce-scatter.3.cloned.1.call-start = ((), (), s32[]{:S(2)}) async-start(), calls=%async_computation.2 | async-start | bytes 5242880 | tf_op jit(solution)/shard_map/reduce_scatter | solution.py:91
  68.1 28.2 %collective-permute-start = (bf16[512,1024]{1,0:T(8,128)(2,1)}, bf16[512,1024]{1,0:T(8,128)(2,1)S(1)}, u32[]{:S(2)}, u32[]{:S(2)}) collective-permute-start(bf16[512,1024]{1,0:T(8,128)(2,1)} %param.15), channel_id=1, source_target_pairs={{0,4},{4,8},{8,12},{12,16},{16,20},{20,24},{24,28},{28,0},{1,5},{5... | collective-permute-start | bytes 3145736 | tf_op jit(solution)/shard_map/ppermute | solution.py:19
  68.4 28.9 %collective-permute-start.1 = (bf16[512,1024]{1,0:T(8,128)(2,1)}, bf16[512,1024]{1,0:T(8,128)(2,1)S(1)}, u32[]{:S(2)}, u32[]{:S(2)}) collective-permute-start(bf16[512,1024]{1,0:T(8,128)(2,1)} %param.15), channel_id=1, source_target_pairs={{0,28},{4,0},{8,4},{12,8},{16,12},{20,16},{24,20},{28,24},{1,29},{... | collective-permute-start | bytes 3145736 | tf_op jit(solution)/shard_map/ppermute | solution.py:22
  96.3 1.0 copy-start.6
  97.3 41.2 %collective-permute-start.2 = (bf16[512,1024]{1,0:T(8,128)(2,1)S(1)}, bf16[512,1024]{1,0:T(8,128)(2,1)S(1)}, u32[]{:S(2)}, u32[]{:S(2)}) collective-permute-start(bf16[512,1024]{1,0:T(8,128)(2,1)S(1)} %collective-permute-done), channel_id=1, source_target_pairs={{0,4},{4,8},{8,12},{12,16},{16,20},{20,24},{24,28},{28,0},{1,5},{5... | collective-permute-start | bytes 3145736 | tf_op jit(solution)/shard_map/ppermute | solution.py:19
  97.3 41.2 %copy-start.8 = (bf16[512,1024]{1,0:T(8,128)(2,1)}, bf16[512,1024]{1,0:T(8,128)(2,1)S(1)}, u32[]{:S(2)}) copy-start(bf16[512,1024]{1,0:T(8,128)(2,1)S(1)} %collective-permute-done.1) | copy-start | bytes 3145732
  97.3 43.6 %collective-permute-start.3 = (bf16[512,1024]{1,0:T(8,128)(2,1)S(1)}, bf16[512,1024]{1,0:T(8,128)(2,1)}, u32[]{:S(2)}, u32[]{:S(2)}) collective-permute-start(bf16[512,1024]{1,0:T(8,128)(2,1)S(1)} %collective-permute-done.1), channel_id=1, source_target_pairs={{0,28},{4,0},{8,4},{12,8},{16,12},{20,16},{24,20},{28,24},{1,29},{... | collective-permute-start | bytes 3145736 | tf_op jit(solution)/shard_map/ppermute | solution.py:22
  138.5 2.4 copy-start.10
  138.5 38.6 %collective-permute-start.4 = (bf16[512,1024]{1,0:T(8,128)(2,1)S(1)}, bf16[512,1024]{1,0:T(8,128)(2,1)}, u32[]{:S(2)}, u32[]{:S(2)}) collective-permute-start(bf16[512,1024]{1,0:T(8,128)(2,1)S(1)} %collective-permute-done.2), channel_id=1, source_target_pairs={{0,4},{4,8},{8,12},{12,16},{16,20},{20,24},{24,28},{28,0},{1,5},{5... | collective-permute-start | bytes 3145736 | tf_op jit(solution)/shard_map/ppermute | solution.py:19
  140.9 41.1 %collective-permute-start.5 = (bf16[512,1024]{1,0:T(8,128)(2,1)}, bf16[512,1024]{1,0:T(8,128)(2,1)}, u32[]{:S(2)}, u32[]{:S(2)}) collective-permute-start(bf16[512,1024]{1,0:T(8,128)(2,1)} %collective-permute-done.3), channel_id=1, source_target_pairs={{0,28},{4,0},{8,4},{12,8},{16,12},{20,16},{24,20},{28,24},{1,29},{... | collective-permute-start | bytes 3145736 | tf_op jit(solution)/shard_map/ppermute | solution.py:22
  177.0 15.4 %collective-permute-start.6 = (bf16[512,1024]{1,0:T(8,128)(2,1)}, bf16[512,1024]{1,0:T(8,128)(2,1)}, u32[]{:S(2)}, u32[]{:S(2)}) collective-permute-start(bf16[512,1024]{1,0:T(8,128)(2,1)} %collective-permute-done.4), channel_id=1, source_target_pairs={{0,4},{4,8},{8,12},{12,16},{16,20},{20,24},{24,28},{28,0},{1,5},{5... | collective-permute-start | bytes 3145736 | tf_op jit(solution)/shard_map/ppermute | solution.py:19
  177.0 1.2 copy-start.5
  177.0 1.5 copy-start.7
  177.0 1.9 copy-start.9
  177.1 2.2 copy-start.11
  178.3 15.5 %copy-start.4 = (bf16[512,8,128]{0,2,1:T(8,128)(2,1)S(1)}, bf16[512,8,128]{0,2,1:T(8,128)(2,1)}, u32[]{:S(2)}) copy-start(bf16[512,8,128]{0,2,1:T(8,128)(2,1)} %copy-done.3) | copy-start | bytes 3145732
  200.0 5.1 %copy-start.2 = (bf16[512,1024]{1,0:T(8,128)(2,1)S(1)}, bf16[512,1024]{1,0:T(8,128)(2,1)}, u32[]{:S(2)}) copy-start(bf16[512,1024]{1,0:T(8,128)(2,1)} %param.12) | copy-start | bytes 3145732
  208.0 18.3 %copy-start.1 = (bf16[512,1024]{0,1:T(8,128)(2,1)S(1)}, bf16[512,1024]{0,1:T(8,128)(2,1)}, u32[]{:S(2)}) copy-start(bf16[512,1024]{0,1:T(8,128)(2,1)} %copy.48) | copy-start | bytes 3145732
Sparse Core Ops, SparseCore 0:
  14.5 30.4 all-gather.4
  46.9 28.6 all-gather.6
  79.0 100.2 reduce-scatter.4
  200.1 75.8 reduce-scatter.2
